TPU v7x, 32 devices: a whole 2x2x4 slice. The times are simulated.
32 devices in a mesh: groups: 2 (over y), frame: 4 (over z), quarter: 2 (over x), sub: 2 (over core).
Axes of the slice: x: 2, y: 2, z: 4, core: 2. Of those that a mesh axis runs over, the one named last changes fastest.
Arguments:
- queries: bfloat16 [16, 1024, 256], P(('groups', 'frame'), ('quarter', 'sub')), parts along dimension 0, may hold values from -36 to 36
- keys: bfloat16 [16, 1024, 256], P(('groups', 'frame'), ('quarter', 'sub')), parts along dimension 0, may hold values from -6 to 6
- values: bfloat16 [16, 1024, 256], P(('groups', 'frame'), ('quarter', 'sub')), parts along dimension 0, may hold values from -6 to 6
Outputs:
- attended: bfloat16 [16, 1024, 256], P(('groups', 'frame'), ('quarter', 'sub')), parts along dimension 0
There are 2 independent parts, one for each index of `groups`. A program takes and returns all parts, laid end to end along the dimension named above; each array names one. Nothing has to cross between parts.
All inputs are finite; a program needn't handle non-finite values.
Results may differ from a plain program's by a relative error of at most 0.0028.
Values may be sent and summed in bfloat16 or wider, within the bound.
A program may use at most 64 MiB of HBM per device.

v0:
```python
import functools
import math

import jax
import jax.numpy as jnp
from jax import lax
from jax.experimental import pallas as pl
from jax.experimental.pallas import tpu as pltpu
from jax.sharding import PartitionSpec as P

STRIP = 16
MESH = pl.DeviceIdType.MESH


def attend(query_rows, key_rows, value_rows, score_scale):
    scores = lax.dot_general(
        query_rows, key_rows, (((1,), (1,)), ((), ())), preferred_element_type=jnp.float32
    )
    highest = jnp.max(scores, axis=-1, keepdims=True)
    expo = jnp.exp((scores - highest) * score_scale)
    totals = jnp.sum(expo, axis=-1, keepdims=True)
    mixed = jnp.dot(expo.astype(jnp.bfloat16), value_rows, preferred_element_type=jnp.float32)
    return (mixed / totals).astype(jnp.bfloat16)


def kernel(
    sizes,
    q_in, k_in, v_in, out,
    q_sp, k_sp, v_sp, q_tm, k_tm, v_tm, o_tm, o_sp,
    local_sem, z_send, z_recv, r_send, r_recv, x_send, x_recv, s_send, s_recv,
):
    n, nq, ns, frames, tokens, width, chunks = sizes
    rows = tokens // n
    rows_chunk = rows // chunks
    score_scale = 1.0 / math.sqrt(width)
    me = lax.axis_index("frame")
    my_quarter = lax.axis_index("quarter")
    my_sub = lax.axis_index("sub")
    temporal_in = (q_in, k_in, v_in)
    temporal_buf = (q_tm, k_tm, v_tm)
    spatial_in = (k_in, v_in)
    spatial_buf = (k_sp, v_sp)
    first = slice(0, width)
    second = slice(width, 2 * width)

    barrier = pltpu.get_barrier_semaphore()
    for step in range(1, n):
        pl.semaphore_signal(
            barrier, inc=1, device_id={"frame": lax.rem(me + step, n)}, device_id_type=MESH
        )
    for step in range(1, nq):
        pl.semaphore_signal(
            barrier, inc=1, device_id={"quarter": lax.rem(my_quarter + step, nq)}, device_id_type=MESH
        )
    for step in range(1, ns):
        pl.semaphore_signal(
            barrier, inc=1, device_id={"sub": lax.rem(my_sub + step, ns)}, device_id_type=MESH
        )

    my_slot = my_quarter * ns + my_sub
    my_rows = pl.ds(pl.multiple_of(me * rows, STRIP), rows)
    my_tokens = pl.ds(pl.multiple_of(my_slot * tokens, tokens), tokens)
    my_frames = pl.ds(me * frames, frames)
    loads = [pltpu.make_async_copy(q_in.at[:, :, first], q_sp, local_sem.at[0])]
    for index in range(2):
        loads.append(
            pltpu.make_async_copy(
                spatial_in[index].at[:, :, first],
                spatial_buf[index].at[:, my_tokens, :],
                local_sem.at[1 + index],
            )
        )
    for index in range(3):
        loads.append(
            pltpu.make_async_copy(
                temporal_in[index].at[:, my_rows, second],
                temporal_buf[index].at[my_frames],
                local_sem.at[3 + index],
            )
        )
    for load in loads:
        load.start()

    pl.semaphore_wait(barrier, (n - 1) + (nq - 1) + (ns - 1))

    low = (me < n // 2).astype(jnp.int32)

    def peer_at(place):
        down = n - 1 - place
        down = down - (down <= me).astype(jnp.int32)
        up = place + (place >= me).astype(jnp.int32)
        return low * down + (1 - low) * up

    def strip_copy(index, chunk, place, target, source):
        lower = pl.multiple_of(target * rows + chunk * rows_chunk, STRIP)
        return pltpu.make_async_remote_copy(
            src_ref=temporal_in[index].at[:, pl.ds(lower, rows_chunk), second],
            dst_ref=temporal_buf[index].at[
                pl.ds(source * frames, frames), pl.ds(chunk * rows_chunk, rows_chunk), :
            ],
            send_sem=z_send.at[(index * chunks + chunk) * n + place],
            recv_sem=z_recv.at[(index * chunks + chunk) * n + source],
            device_id={"frame": target},
            device_id_type=MESH,
        )

    def return_copy(chunk, place, target, source):
        lower = pl.multiple_of(source * rows + chunk * rows_chunk, STRIP)
        return pltpu.make_async_remote_copy(
            src_ref=o_tm.at[
                pl.ds(target * frames, frames), pl.ds(chunk * rows_chunk, rows_chunk), :
            ],
            dst_ref=out.at[:, pl.ds(lower, rows_chunk), second],
            send_sem=r_send.at[chunk * n + place],
            recv_sem=r_recv.at[chunk * n + source],
            device_id={"frame": target},
            device_id_type=MESH,
        )

    def quarter_copy(index, frame, step, target, source):
        place = pl.ds(pl.multiple_of((source * ns + my_sub) * tokens, tokens), tokens)
        return pltpu.make_async_remote_copy(
            src_ref=spatial_in[index].at[frame, :, first],
            dst_ref=spatial_buf[index].at[frame, place, :],
            send_sem=x_send.at[(index * frames + frame) * nq + step],
            recv_sem=x_recv.at[(index * frames + frame) * nq + source],
            device_id={"quarter": target},
            device_id_type=MESH,
        )

    def sub_copy(index, frame, step, quarter_step, target, quarter, source):
        place = pl.ds(pl.multiple_of((quarter * ns + source) * tokens, tokens), tokens)
        landed = spatial_buf[index].at[frame, place, :]
        return pltpu.make_async_remote_copy(
            src_ref=spatial_in[index].at[frame, :, first] if quarter_step == 0 else landed,
            dst_ref=landed,
            send_sem=s_send.at[((index * frames + frame) * nq + quarter_step) * ns + step],
            recv_sem=s_recv.at[((index * frames + frame) * nq + quarter) * ns + source],
            device_id={"sub": target},
            device_id_type=MESH,
        )

    sent = []
    for place in range(n - 1):
        for chunk in range(chunks):
            for index in range(3):
                sent.append(strip_copy(index, chunk, place, peer_at(place), me))
                sent[-1].start()
    for frame in range(frames):
        for index in range(2):
            for step in range(1, nq):
                sent.append(
                    quarter_copy(index, frame, step, lax.rem(my_quarter + step, nq), my_quarter)
                )
                sent[-1].start()
            for step in range(1, ns):
                sent.append(
                    sub_copy(
                        index, frame, step, 0, lax.rem(my_sub + step, ns), my_quarter, my_sub
                    )
                )
                sent[-1].start()
    for load in loads:
        load.wait()

    def forward(frame):
        for step in range(1, nq):
            source = lax.rem(my_quarter + step, nq)
            for index in range(2):
                quarter_copy(index, frame, step, source, source).wait_recv()
                for hop in range(1, ns):
                    sent.append(
                        sub_copy(
                            index, frame, hop, step, lax.rem(my_sub + hop, ns), source, my_sub
                        )
                    )
                    sent[-1].start()

    def spatial_frame(frame):
        for quarter_step in range(nq):
            quarter = lax.rem(my_quarter + quarter_step, nq)
            for step in range(1, ns):
                source = lax.rem(my_sub + step, ns)
                for index in range(2):
                    sub_copy(
                        index, frame, step, quarter_step, source, quarter, source
                    ).wait_recv()
        o_sp[frame] = attend(q_sp[frame], k_sp[frame], v_sp[frame], score_scale)
        put = pltpu.make_async_copy(
            o_sp.at[frame], out.at[frame, :, first], local_sem.at[6 + frame]
        )
        put.start()
        return put

    def temporal_chunk(chunk):
        for place in range(n - 1):
            source = peer_at(place)
            for index in range(3):
                strip_copy(index, chunk, place, source, source).wait_recv()
        for lower in range(chunk * rows_chunk, (chunk + 1) * rows_chunk, STRIP):
            strip = [
                buffer[:, lower : lower + STRIP, :].reshape(n * frames * STRIP, width)
                for buffer in temporal_buf
            ]
            mixed = attend(*strip, score_scale)
            o_tm[:, lower : lower + STRIP, :] = mixed.reshape(n * frames, STRIP, width)
        for place in range(n - 1):
            sent.append(return_copy(chunk, place, peer_at(place), me))
            sent[-1].start()
        lower = pl.multiple_of(me * rows + chunk * rows_chunk, STRIP)
        put = pltpu.make_async_copy(
            o_tm.at[my_frames, pl.ds(chunk * rows_chunk, rows_chunk), :],
            out.at[:, pl.ds(lower, rows_chunk), second],
            local_sem.at[6 + frames + chunk],
        )
        put.start()
        return put

    puts = []
    forward(0)
    puts.append(spatial_frame(0))
    for frame in range(1, frames):
        forward(frame)
    puts.append(temporal_chunk(0))
    for chunk in range(1, chunks):
        puts.append(temporal_chunk(chunk))
    for frame in range(1, frames):
        puts.append(spatial_frame(frame))
    for chunk in range(chunks):
        for place in range(n - 1):
            source = peer_at(place)
            return_copy(chunk, place, source, source).wait_recv()
    for put in puts:
        put.wait()
    for copy in sent:
        copy.wait_send()


def body(mesh, queries, keys, values):
    frames, tokens, both = queries.shape
    width = both // 2
    n, nq, ns = mesh.shape["frame"], mesh.shape["quarter"], mesh.shape["sub"]
    chunks = math.gcd(tokens // (STRIP * n), 2)
    rows = tokens // n
    bf16 = jnp.bfloat16
    dma = pltpu.SemaphoreType.DMA
    spatial = pltpu.VMEM((frames, nq * ns * tokens, width), bf16)
    temporal = pltpu.VMEM((n * frames, rows, width), bf16)
    own = pltpu.VMEM((frames, tokens, width), bf16)
    return pl.pallas_call(
        functools.partial(kernel, (n, nq, ns, frames, tokens, width, chunks)),
        out_shape=jax.ShapeDtypeStruct(queries.shape, bf16),
        in_specs=[pl.BlockSpec(memory_space=pltpu.HBM)] * 3,
        out_specs=pl.BlockSpec(memory_space=pl.ANY),
        scratch_shapes=[
            own, spatial, spatial, temporal, temporal, temporal, temporal, own,
            dma((6 + frames + chunks,)),
            dma((3 * chunks * n,)), dma((3 * chunks * n,)),
            dma((chunks * n,)), dma((chunks * n,)),
            dma((2 * frames * nq,)), dma((2 * frames * nq,)),
            dma((2 * frames * nq * ns,)), dma((2 * frames * nq * ns,)),
        ],
        compiler_params=pltpu.CompilerParams(collective_id=0, has_side_effects=True, vmem_limit_bytes=24 << 20),
    )(*[pltpu.with_memory_space_constraint(a, pltpu.HBM) for a in (queries, keys, values)])


def solution(mesh):
    spec = P(("groups", "frame"), ("quarter", "sub"), None)
    return jax.shard_map(
        functools.partial(body, mesh),
        mesh=mesh,
        in_specs=(spec, spec, spec),
        out_specs=spec,
        check_vma=False,
    )
```

profile of v0, /device:TPU:0, one launch (start us, length us, event | category | flops | bytes accessed | tf_op | source)
XLA Modules:
  0.0 20.5 jit_solution(13606172429115263000)
XLA Ops:
  0.0 19.8 %shard_map.37 = bf16[2,256,256]{2,1,0:T(8,128)(2,1)S(1)} custom-call(bf16[2,256,256]{2,1,0:T(8,128)(2,1)} %q_in.1, bf16[2,256,256]{2,1,0:T(8,128)(2,1)} %k_in.1, bf16[2,256,256]{2,1,0:T(8,128)(2,1)} %v_in.1), custom_call_target="tpu_custom_call" | custom-call | tf_op jit(solution)/shard_map/pallas_call | solution.py:250
  19.8 0.7 %copy.5 = bf16[2,256,256]{2,1,0:T(8,128)(2,1)} copy(bf16[2,256,256]{2,1,0:T(8,128)(2,1)S(1)} %shard_map.37) | data formatting | bytes 524288
where the time goes:
time: 20.7 us; the launch traced here: 20.5 us
  Pallas kernels  19.8 us (96%)
  local copies, waits for them, and re-layouts  0.71 us (3%)
    pallas_call x1, Pallas kernels, body(): pl.pallas_call(functools.partial(kernel, (n, nq, ns, frames, tokens, widt...  19.8 us
    unnamed x1, local copies, waits for them, and re-layouts  0.71 us

commit v1 on v0

v1 whole, which is shorter than its diff:
```python
import functools
import math

import jax
import jax.numpy as jnp
from jax import lax
from jax.experimental import pallas as pl
from jax.experimental.pallas import tpu as pltpu
from jax.sharding import PartitionSpec as P

STRIP = 16
MESH = pl.DeviceIdType.MESH


def attend(query_rows, key_rows, value_rows, score_scale):
    scores = lax.dot_general(
        query_rows, key_rows, (((1,), (1,)), ((), ())), preferred_element_type=jnp.float32
    )
    highest = jnp.max(scores, axis=-1, keepdims=True)
    expo = jnp.exp((scores - highest) * score_scale)
    totals = jnp.sum(expo, axis=-1, keepdims=True)
    mixed = jnp.dot(expo.astype(jnp.bfloat16), value_rows, preferred_element_type=jnp.float32)
    return (mixed / totals).astype(jnp.bfloat16)


def attend_strips(keys, values, queries, score_scale):
    width = keys.shape[-1]
    strips = [slice(lower, lower + STRIP) for lower in range(0, keys.shape[1], STRIP)]
    scores = jnp.concatenate(
        [
            lax.dot_general(
                queries[:, strip].reshape(-1, width), keys[:, strip].reshape(-1, width),
                (((1,), (1,)), ((), ())), preferred_element_type=jnp.float32,
            )
            for strip in strips
        ]
    )
    highest = jnp.max(scores, axis=-1, keepdims=True)
    expo = jnp.exp((scores - highest) * score_scale)
    totals = jnp.sum(expo, axis=-1, keepdims=True)
    weights = expo.astype(jnp.bfloat16)
    count = queries.shape[0] * STRIP
    mixed = [
        jnp.dot(
            weights[place * count : (place + 1) * count], values[:, strip].reshape(-1, width),
            preferred_element_type=jnp.float32,
        )
        for place, strip in enumerate(strips)
    ]
    result = (jnp.concatenate(mixed) / totals).astype(jnp.bfloat16)
    return [result[place * count : (place + 1) * count] for place in range(len(strips))]


def wait_for(ref, sem):
    pltpu.make_async_copy(ref, ref, sem).wait()


def kernel(
    sizes,
    q_in, k_in, v_in, out,
    q_sp, kv_sp, tm, o_tm, o_sp,
    in_z, in_x, in_s,
    local_sem, z_send, z_recv, r_send, r_recv,
    x_send, x_recv, s_send, s_recv,
):
    n, nq, ns, frames, tokens, width, parts = sizes
    chunks = len(parts)
    starts = [sum(parts[:chunk]) for chunk in range(chunks)]
    rows = tokens // n
    score_scale = 1.0 / math.sqrt(width)
    me = lax.axis_index("frame")
    my_quarter = lax.axis_index("quarter")
    my_sub = lax.axis_index("sub")
    arrays = (q_in, k_in, v_in)
    first = slice(0, width)
    second = slice(width, 2 * width)
    my_frames = pl.ds(me * frames, frames)
    my_spatial = kv_sp.at[:, :, my_quarter, my_sub]
    axes = (("frame", me, n, in_z), ("quarter", my_quarter, nq, in_x), ("sub", my_sub, ns, in_s))

    barrier = pltpu.get_barrier_semaphore()
    for name, place, extent, _ in axes:
        for other in range(1, extent):
            @pl.when(other > place)
            def _(name=name, other=other):
                pl.semaphore_signal(barrier, inc=1, device_id={name: other}, device_id_type=MESH)

    below = me + my_quarter + my_sub

    @pl.when(below > 0)
    def _():
        pl.semaphore_wait(barrier, below)

    for name, place, extent, answers in axes:
        for other in range(extent - 1):
            @pl.when(other < place)
            def _(name=name, other=other, place=place, answers=answers):
                pl.semaphore_signal(
                    answers.at[place], inc=1, device_id={name: other}, device_id_type=MESH
                )

    def send_strips(owner):
        for chunk in range(chunks):
            for index in range(3):
                lower = owner * rows + starts[chunk]
                pltpu.make_async_remote_copy(
                    src_ref=arrays[index].at[:, lower : lower + parts[chunk], second],
                    dst_ref=tm.at[index, my_frames, pl.ds(starts[chunk], parts[chunk]), :],
                    send_sem=z_send.at[0],
                    recv_sem=z_recv.at[chunk],
                    device_id={"frame": owner},
                    device_id_type=MESH,
                ).start()

    for owner in range(n - 1):
        @pl.when(owner < me)
        def _(owner=owner):
            send_strips(owner)

    loads = [
        (q_in.at[:, :, first], q_sp, local_sem.at[0]),
        (k_in.at[:, :, first], kv_sp.at[0, :, my_quarter, my_sub], local_sem.at[1]),
        (v_in.at[:, :, first], kv_sp.at[1, :, my_quarter, my_sub], local_sem.at[1]),
    ]
    my_rows = pl.ds(pl.multiple_of(me * rows, STRIP), rows)
    for index in range(3):
        loads.append((arrays[index].at[:, my_rows, second], tm.at[index, my_frames], local_sem.at[2]))
    for load in loads:
        pltpu.make_async_copy(*load).start()

    for name, place, extent, answers in axes[1:]:
        for other in range(1, extent):
            @pl.when(other > place)
            def _(other=other, answers=answers):
                pl.semaphore_wait(answers.at[other], 1)

    def quarter_copy(index, frame, step):
        return pltpu.make_async_remote_copy(
            src_ref=arrays[index + 1].at[frame, :, first],
            dst_ref=kv_sp.at[index, frame, my_quarter, my_sub],
            send_sem=x_send.at[step - 1],
            recv_sem=x_recv.at[frame * (nq - 1) + step - 1],
            device_id={"quarter": lax.rem(my_quarter + step, nq)},
            device_id_type=MESH,
        )

    def sub_copy(index, frame, hop, quarter, source):
        return pltpu.make_async_remote_copy(
            src_ref=source,
            dst_ref=kv_sp.at[index, frame, quarter, my_sub],
            send_sem=s_send.at[hop - 1],
            recv_sem=s_recv.at[frame * (ns - 1) + hop - 1],
            device_id={"sub": lax.rem(my_sub + hop, ns)},
            device_id_type=MESH,
        )

    for frame in range(frames):
        for index in range(2):
            for step in range(1, nq):
                quarter_copy(index, frame, step).start()
            for hop in range(1, ns):
                source = arrays[index + 1].at[frame, :, first]
                sub_copy(index, frame, hop, my_quarter, source).start()

    for owner in range(1, n):
        @pl.when(owner > me)
        def _(owner=owner):
            pl.semaphore_wait(in_z.at[owner], 1)
            send_strips(owner)

    wait_for(q_sp, local_sem.at[0])
    wait_for(my_spatial, local_sem.at[1])
    wait_for(tm.at[:, my_frames], local_sem.at[2])

    def forward(frame):
        for step in range(1, nq):
            source = lax.rem(my_quarter + step, nq)
            landed = kv_sp.at[:, frame, source, my_sub]
            wait_for(landed, x_recv.at[frame * (nq - 1) + nq - step - 1])
            for index in range(2):
                for hop in range(1, ns):
                    sub_copy(index, frame, hop, source, kv_sp.at[index, frame, source, my_sub]).start()

    puts = []

    def put(source, target):
        puts.append(pltpu.make_async_copy(source, target, local_sem.at[3 + len(puts)]))
        puts[-1].start()

    def spatial_frame(frame):
        for step in range(1, ns):
            source = lax.rem(my_sub + step, ns)
            wait_for(kv_sp.at[:, frame, :, source], s_recv.at[frame * (ns - 1) + ns - step - 1])
        key_rows = kv_sp[0, frame].reshape(nq * ns * tokens, width)
        value_rows = kv_sp[1, frame].reshape(nq * ns * tokens, width)
        o_sp[frame] = attend(q_sp[frame], key_rows, value_rows, score_scale)
        put(o_sp.at[frame], out.at[frame, :, first])

    def temporal_chunk(chunk):
        here = slice(starts[chunk], starts[chunk] + parts[chunk])
        wait_for(tm.at[:, pl.ds(0, (n - 1) * frames), here], z_recv.at[chunk])
        block = tm[1, :, here, :], tm[2, :, here, :], tm[0, :, here, :]
        for place, mixed in enumerate(attend_strips(*block, score_scale)):
            strip = slice(starts[chunk] + place * STRIP, starts[chunk] + (place + 1) * STRIP)
            o_tm[:, strip, :] = mixed.reshape(n * frames, STRIP, width)
        lower = pl.multiple_of(me * rows + starts[chunk], STRIP)
        target = out.at[:, pl.ds(lower, parts[chunk]), second]
        for receiver in range(n):
            @pl.when(receiver != me)
            def _(receiver=receiver):
                pltpu.make_async_remote_copy(
                    src_ref=o_tm.at[pl.ds(receiver * frames, frames), here],
                    dst_ref=target,
                    send_sem=r_send.at[0],
                    recv_sem=r_recv.at[0],
                    device_id={"frame": receiver},
                    device_id_type=MESH,
                ).start()
        put(o_tm.at[my_frames, here], target)

    forward(0)
    spatial_frame(0)
    for frame in range(1, frames):
        forward(frame)
    for chunk in range(chunks):
        temporal_chunk(chunk)
    for frame in range(1, frames):
        spatial_frame(frame)

    others = pl.ds(0, (n - 1) * frames)
    wait_for(o_tm.at[others], r_recv.at[0])
    for copy in puts:
        copy.wait()
    wait_for(tm.at[:, others], z_send.at[0])
    wait_for(o_tm.at[others], r_send.at[0])
    for step in range(1, nq):
        wait_for(my_spatial, x_send.at[step - 1])
    for hop in range(1, ns):
        wait_for(kv_sp.at[:, :, :, my_sub], s_send.at[hop - 1])


def body(mesh, queries, keys, values):
    frames, tokens, both = queries.shape
    width = both // 2
    n, nq, ns = mesh.shape["frame"], mesh.shape["quarter"], mesh.shape["sub"]
    rows = tokens // n
    parts = (rows,)
    chunks = len(parts)
    bf16 = jnp.bfloat16
    dma = pltpu.SemaphoreType.DMA
    regular = pltpu.SemaphoreType.REGULAR
    own = pltpu.VMEM((frames, tokens, width), bf16)
    return pl.pallas_call(
        functools.partial(kernel, (n, nq, ns, frames, tokens, width, parts)),
        out_shape=jax.ShapeDtypeStruct(queries.shape, bf16),
        in_specs=[pl.BlockSpec(memory_space=pltpu.HBM)] * 3,
        out_specs=pl.BlockSpec(memory_space=pl.ANY),
        scratch_shapes=[
            own,
            pltpu.VMEM((2, frames, nq, ns, tokens, width), bf16),
            pltpu.VMEM((3, n * frames, rows, width), bf16),
            pltpu.VMEM((n * frames, rows, width), bf16),
            own,
            regular((n,)), regular((nq,)), regular((ns,)),
            dma((3 + frames + chunks,)),
            dma((1,)), dma((chunks,)), dma((1,)), dma((1,)),
            dma((nq - 1,)), dma((frames * (nq - 1),)),
            dma((ns - 1,)), dma((frames * (ns - 1),)),
        ],
        compiler_params=pltpu.CompilerParams(collective_id=0, has_side_effects=True, vmem_limit_bytes=24 << 20),
    )(*[pltpu.with_memory_space_constraint(a, pltpu.HBM) for a in (queries, keys, values)])


def solution(mesh):
    spec = P(("groups", "frame"), ("quarter", "sub"), None)
    return jax.shard_map(
        functools.partial(body, mesh),
        mesh=mesh,
        in_specs=(spec, spec, spec),
        out_specs=spec,
        check_vma=False,
    )
```

time: 20.7 us -> 20.2 us (0.976)
  Pallas kernels: 19.8 us -> 19.3 us
    pallas_call x1, Pallas kernels: 19.8 us -> 19.3 us  [body(): pl.pallas_call(functools.partial(kernel, (n, nq, ns, frames, tokens, widt...]
where the time goes in v1:
time: 20.2 us; the launch traced here: 20.1 us
  Pallas kernels  19.3 us (96%)
  local copies, waits for them, and re-layouts  0.71 us (4%)
    pallas_call x1, Pallas kernels, body(): pl.pallas_call(functools.partial(kernel, (n, nq, ns, frames, tokens, widt...  19.3 us
    unnamed x1, local copies, waits for them, and re-layouts  0.71 us

profile of v1, /device:TPU:0, one launch (start us, length us, event | category | flops | bytes accessed | tf_op | source)
XLA Modules:
  0.0 20.1 jit_solution(10547220833467869659)
XLA Ops:
  0.0 19.3 %shard_map.37 = bf16[2,256,256]{2,1,0:T(8,128)(2,1)S(1)} custom-call(bf16[2,256,256]{2,1,0:T(8,128)(2,1)} %q_in.1, bf16[2,256,256]{2,1,0:T(8,128)(2,1)} %k_in.1, bf16[2,256,256]{2,1,0:T(8,128)(2,1)} %v_in.1), custom_call_target="tpu_custom_call" | custom-call | tf_op jit(solution)/shard_map/pallas_call | solution.py:253
  19.4 0.7 %copy.5 = bf16[2,256,256]{2,1,0:T(8,128)(2,1)} copy(bf16[2,256,256]{2,1,0:T(8,128)(2,1)S(1)} %shard_map.37) | data formatting | bytes 524288

commit v2 on v1

--- a/solution.py
+++ b/solution.py
@@ -60,17 +60,21 @@
     q_in, k_in, v_in, out,
     q_sp, kv_sp, tm, o_tm, o_sp,
     in_z, in_x, in_s,
-    local_sem, z_send, z_recv, r_send, r_recv,
+    local_sem, cross_send, cross_recv, own_send, own_recv, r_send, r_recv,
     x_send, x_recv, s_send, s_recv,
 ):
     n, nq, ns, frames, tokens, width, parts = sizes
     chunks = len(parts)
     starts = [sum(parts[:chunk]) for chunk in range(chunks)]
-    rows = tokens // n
+    half = n // 2
+    rows = tokens // half
     score_scale = 1.0 / math.sqrt(width)
     me = lax.axis_index("frame")
     my_quarter = lax.axis_index("quarter")
     my_sub = lax.axis_index("sub")
+    upper = (me >= half).astype(jnp.int32)
+    base = upper * half
+    mine = me - base
     arrays = (q_in, k_in, v_in)
     first = slice(0, width)
     second = slice(width, 2 * width)
@@ -99,30 +103,61 @@
                     answers.at[place], inc=1, device_id={name: other}, device_id_type=MESH
                 )
 
-    def send_strips(owner):
+    def strip_copy(index, chunk, owner, send_sem, recv_sem):
+        lower = lax.rem(owner, half) * rows + starts[chunk]
+        return pltpu.make_async_remote_copy(
+            src_ref=arrays[index].at[:, pl.ds(pl.multiple_of(lower, STRIP), parts[chunk]), second],
+            dst_ref=tm.at[index, my_frames, pl.ds(starts[chunk], parts[chunk]), :],
+            send_sem=send_sem,
+            recv_sem=recv_sem,
+            device_id={"frame": owner},
+            device_id_type=MESH,
+        )
+
+    down = [(owner, chunk) for owner in range(half - 1, -1, -1) for chunk in range(chunks)]
+    up = [(owner, chunk) for owner in range(n - 1, half - 1, -1) for chunk in range(chunks)]
+    up.insert(0, up.pop(up.index((half, 0))))
+
+    def send_cross(entries, known):
+        for owner, chunk in entries:
+            if owner not in known:
+                pl.semaphore_wait(in_z.at[owner], 1)
+                known.add(owner)
+            for index in (1, 2):
+                strip_copy(index, chunk, owner, cross_send.at[0], cross_recv.at[chunk]).start()
+
+    soon, later = down[: len(down) // 2], down[len(down) // 2 :]
+    below_half = set(range(half))
+
+    @pl.when(upper == 1)
+    def _():
+        send_cross(soon, below_half)
+
+    @pl.when((upper == 1) & (my_sub == 0))
+    def _():
+        send_cross(later, below_half)
+
+    def neighbour(step):
+        return base + lax.rem(mine + step, half)
+
+    for step in range(1, half):
+        @pl.when(neighbour(step) > me)
+        def _(step=step):
+            pl.semaphore_wait(in_z.at[neighbour(step)], 1)
+
         for chunk in range(chunks):
             for index in range(3):
-                lower = owner * rows + starts[chunk]
-                pltpu.make_async_remote_copy(
-                    src_ref=arrays[index].at[:, lower : lower + parts[chunk], second],
-                    dst_ref=tm.at[index, my_frames, pl.ds(starts[chunk], parts[chunk]), :],
-                    send_sem=z_send.at[0],
-                    recv_sem=z_recv.at[chunk],
-                    device_id={"frame": owner},
-                    device_id_type=MESH,
+                strip_copy(
+                    index, chunk, neighbour(step),
+                    own_send.at[step - 1], own_recv.at[chunk * (half - 1) + step - 1],
                 ).start()
-
-    for owner in range(n - 1):
-        @pl.when(owner < me)
-        def _(owner=owner):
-            send_strips(owner)
 
     loads = [
         (q_in.at[:, :, first], q_sp, local_sem.at[0]),
         (k_in.at[:, :, first], kv_sp.at[0, :, my_quarter, my_sub], local_sem.at[1]),
         (v_in.at[:, :, first], kv_sp.at[1, :, my_quarter, my_sub], local_sem.at[1]),
     ]
-    my_rows = pl.ds(pl.multiple_of(me * rows, STRIP), rows)
+    my_rows = pl.ds(pl.multiple_of(mine * rows, STRIP), rows)
     for index in range(3):
         loads.append((arrays[index].at[:, my_rows, second], tm.at[index, my_frames], local_sem.at[2]))
     for load in loads:
@@ -162,11 +197,13 @@
                 source = arrays[index + 1].at[frame, :, first]
                 sub_copy(index, frame, hop, my_quarter, source).start()
 
-    for owner in range(1, n):
-        @pl.when(owner > me)
-        def _(owner=owner):
-            pl.semaphore_wait(in_z.at[owner], 1)
-            send_strips(owner)
+    @pl.when((upper == 1) & (my_sub > 0))
+    def _():
+        send_cross(later, below_half)
+
+    @pl.when(upper == 0)
+    def _():
+        send_cross(up, set())
 
     wait_for(q_sp, local_sem.at[0])
     wait_for(my_spatial, local_sem.at[1])
@@ -198,53 +235,68 @@
 
     def temporal_chunk(chunk):
         here = slice(starts[chunk], starts[chunk] + parts[chunk])
-        wait_for(tm.at[:, pl.ds(0, (n - 1) * frames), here], z_recv.at[chunk])
-        block = tm[1, :, here, :], tm[2, :, here, :], tm[0, :, here, :]
+        for step in range(1, half):
+            sender = pl.ds(neighbour(step) * frames, frames)
+            wait_for(tm.at[:, sender, here], own_recv.at[chunk * (half - 1) + half - step - 1])
+        wait_for(
+            tm.at[1:3, pl.ds((half - base) * frames, half * frames), here], cross_recv.at[chunk]
+        )
+        asked = pl.ds(base * frames, half * frames)
+        block = tm[1, :, here, :], tm[2, :, here, :], tm[0, asked, here, :]
         for place, mixed in enumerate(attend_strips(*block, score_scale)):
             strip = slice(starts[chunk] + place * STRIP, starts[chunk] + (place + 1) * STRIP)
-            o_tm[:, strip, :] = mixed.reshape(n * frames, STRIP, width)
-        lower = pl.multiple_of(me * rows + starts[chunk], STRIP)
+            o_tm[:, strip, :] = mixed.reshape(half * frames, STRIP, width)
+        lower = pl.multiple_of(mine * rows + starts[chunk], STRIP)
         target = out.at[:, pl.ds(lower, parts[chunk]), second]
-        for receiver in range(n):
-            @pl.when(receiver != me)
-            def _(receiver=receiver):
-                pltpu.make_async_remote_copy(
-                    src_ref=o_tm.at[pl.ds(receiver * frames, frames), here],
-                    dst_ref=target,
-                    send_sem=r_send.at[0],
-                    recv_sem=r_recv.at[0],
-                    device_id={"frame": receiver},
-                    device_id_type=MESH,
-                ).start()
-        put(o_tm.at[my_frames, here], target)
+        for step in range(1, half):
+            receiver = lax.rem(mine + step, half)
+            pltpu.make_async_remote_copy(
+                src_ref=o_tm.at[pl.ds(receiver * frames, frames), here],
+                dst_ref=target,
+                send_sem=r_send.at[step - 1],
+                recv_sem=r_recv.at[step - 1],
+                device_id={"frame": neighbour(step)},
+                device_id_type=MESH,
+            ).start()
+        put(o_tm.at[pl.ds(mine * frames, frames), here], target)
 
     forward(0)
     spatial_frame(0)
     for frame in range(1, frames):
         forward(frame)
-    for chunk in range(chunks):
-        temporal_chunk(chunk)
+    temporal_chunk(0)
     for frame in range(1, frames):
         spatial_frame(frame)
-
-    others = pl.ds(0, (n - 1) * frames)
-    wait_for(o_tm.at[others], r_recv.at[0])
+    for chunk in range(1, chunks):
+        temporal_chunk(chunk)
+
+    for step in range(1, half):
+        lower = pl.multiple_of(lax.rem(mine + step, half) * rows, STRIP)
+        wait_for(out.at[:, pl.ds(lower, rows), second], r_recv.at[half - step - 1])
     for copy in puts:
         copy.wait()
-    wait_for(tm.at[:, others], z_send.at[0])
-    wait_for(o_tm.at[others], r_send.at[0])
+    wait_for(my_spatial, cross_send.at[0])
+    for step in range(1, half):
+        wait_for(tm.at[:, my_frames], own_send.at[step - 1])
+        wait_for(o_tm.at[pl.ds(0, frames)], r_send.at[step - 1])
     for step in range(1, nq):
         wait_for(my_spatial, x_send.at[step - 1])
     for hop in range(1, ns):
         wait_for(kv_sp.at[:, :, :, my_sub], s_send.at[hop - 1])
 
 
+def split_rows(rows):
+    pieces = math.gcd(rows // STRIP, 4)
+    return (rows // pieces,) * pieces
+
+
 def body(mesh, queries, keys, values):
     frames, tokens, both = queries.shape
     width = both // 2
     n, nq, ns = mesh.shape["frame"], mesh.shape["quarter"], mesh.shape["sub"]
-    rows = tokens // n
-    parts = (rows,)
+    half = n // 2
+    rows = tokens // half
+    parts = split_rows(rows)
     chunks = len(parts)
     bf16 = jnp.bfloat16
     dma = pltpu.SemaphoreType.DMA
@@ -259,11 +311,13 @@
             own,
             pltpu.VMEM((2, frames, nq, ns, tokens, width), bf16),
             pltpu.VMEM((3, n * frames, rows, width), bf16),
-            pltpu.VMEM((n * frames, rows, width), bf16),
+            pltpu.VMEM((half * frames, rows, width), bf16),
             own,
             regular((n,)), regular((nq,)), regular((ns,)),
             dma((3 + frames + chunks,)),
-            dma((1,)), dma((chunks,)), dma((1,)), dma((1,)),
+            dma((1,)), dma((chunks,)),
+            dma((half - 1,)), dma((chunks * (half - 1),)),
+            dma((half - 1,)), dma((half - 1,)),
             dma((nq - 1,)), dma((frames * (nq - 1),)),
             dma((ns - 1,)), dma((frames * (ns - 1),)),
         ],

time: 20.2 us -> 19.9 us (0.985)
  Pallas kernels: 19.3 us -> 19 us
    pallas_call x1, Pallas kernels: 19.3 us -> 19 us  [body(): pl.pallas_call(functools.partial(kernel, (n, nq, ns, frames, tokens, widt...]
where the time goes in v2:
time: 19.9 us; the launch traced here: 19.7 us
  Pallas kernels  19 us (95%)
  local copies, waits for them, and re-layouts  0.71 us (4%)
    pallas_call x1, Pallas kernels, body(): pl.pallas_call(functools.partial(kernel, (n, nq, ns, frames, tokens, widt...  19 us
    unnamed x1, local copies, waits for them, and re-layouts  0.71 us

profile of v2, /device:TPU:0, one launch (start us, length us, event | category | flops | bytes accessed | tf_op | source)
XLA Modules:
  0.0 19.7 jit_solution(14425128242409440653)
XLA Ops:
  0.0 19.0 %shard_map.37 = bf16[2,256,256]{2,1,0:T(8,128)(2,1)S(1)} custom-call(bf16[2,256,256]{2,1,0:T(8,128)(2,1)} %q_in.1, bf16[2,256,256]{2,1,0:T(8,128)(2,1)} %k_in.1, bf16[2,256,256]{2,1,0:T(8,128)(2,1)} %v_in.1), custom_call_target="tpu_custom_call" | custom-call | tf_op jit(solution)/shard_map/pallas_call | solution.py:305
  19.0 0.7 %copy.5 = bf16[2,256,256]{2,1,0:T(8,128)(2,1)} copy(bf16[2,256,256]{2,1,0:T(8,128)(2,1)S(1)} %shard_map.37) | data formatting | bytes 524288
